TPU v7x, 32 devices: a whole 2x2x4 slice. The times are simulated.
32 devices in a mesh: shape: 8 (over z, x), cls: 4 (over y, core).
Axes of the slice: x: 2, y: 2, z: 4, core: 2. Of those that a mesh axis runs over, the one named last changes fastest.
Arguments:
- shapes: bfloat16 [4096, 1280], P('shape', 'cls'), may hold values from -600 to 600
- classes: bfloat16 [20480, 1280], P('cls'), may hold values from -400 to 400
- counts: int32 [20480], P('cls'), may hold values from 0 to 2, as said below
Outputs:
- assignment: bfloat16 [4096, 20480], P('shape', 'cls')
Inputs may be any that keep to these rules, and one draw needn't show every extreme that they name: The counts sum to 4096; exactly 1024 classes have count 2.
All inputs are finite; a program needn't handle non-finite values.
Results may differ from a plain program's by a relative error of at most 0.001.
Values may be sent and summed in bfloat16 or wider, within the bound.
No kernel may reach another device: no remote copies, remote signals or barrier semaphores. Data moves between devices by JAX's collectives and lax.ppermute only.
A program may use at most 128 MiB of HBM per device.

v0:
```python
import jax
import jax.numpy as jnp
from jax import lax
from jax.sharding import PartitionSpec as P

ITERS = 3
logit_scale = 40.0
epsilon = 1e-06


def row_totals(partial_value):
    return lax.psum(partial_value, "cls")


def shards(shapes, classes, counts):
    class_f = classes.astype(jnp.float32)
    class_scale = lax.rsqrt(jnp.sum(class_f * class_f, axis=1) + epsilon)
    piece = lax.all_gather(shapes, "cls", axis=1, tiled=True)
    term = lax.dot_general(
        piece, classes, (((1,), (1,)), ((), ())), preferred_element_type=jnp.float32
    )
    piece_f = piece.astype(jnp.float32)
    squares = jnp.sum(piece_f * piece_f, axis=1)
    shape_scale = lax.rsqrt(squares + epsilon)
    kernel = jnp.exp(logit_scale * term * shape_scale[:, None] * class_scale[None, :])
    target = counts.astype(jnp.float32)
    row_inv = 1.0 / row_totals(jnp.sum(kernel, axis=1))
    col_scale = jnp.zeros((classes.shape[0],), jnp.float32)
    for step in range(ITERS):
        column_part = jnp.dot(row_inv, kernel, precision=lax.Precision.HIGHEST)
        col_scale = target / lax.psum(column_part, "shape")
        row_inv = 1.0 / row_totals(jnp.dot(kernel, col_scale, precision=lax.Precision.HIGHEST))
    result = row_inv[:, None] * kernel * col_scale[None, :]
    return result.astype(jnp.bfloat16)


def solution(mesh):
    placed = (P("shape", "cls"), P("cls", None), P("cls"))
    return jax.shard_map(
        shards, mesh=mesh, in_specs=placed, out_specs=P("shape", "cls"), check_vma=False
    )
```

profile of v0, /device:TPU:0, one launch (start us, length us, event | category | flops | bytes accessed | tf_op | source)
XLA Modules:
  0.0 246.2 jit_solution(15459654316340277970)
XLA Ops:
  6.5 0.0 all-gather.2.cloned.1.call-start
  6.5 0.7 all-gather.2.cloned.1.call-update
  7.3 7.3 %multiply_reduce_fusion = f32[5120]{0:T(1024)S(1)} fusion(bf16[5120,1280]{1,0:T(8,128)(2,1)} %param.4), kind=kLoop, calls=%fused_computation | loop fusion | flops 19655680 | bytes 13127680 | tf_op jit(solution)/shard_map/reduce_sum | solution.py:17
  14.6 15.2 %all-gather.2.cloned.1.call-done = bf16[512,1280]{0,1:T(8,128)(2,1)} async-done(((bf16[512,320]{0,1:T(8,128)(2,1)}), bf16[512,1280]{0,1:T(8,128)(2,1)}) %all-gather.2.cloned.1.call-update) | async-done | bytes 1310736 | tf_op jit(solution)/shard_map/all_gather | solution.py:18
  29.8 1.7 multiply_reduce_fusion.1
  31.5 16.2 %fusion = (f32[512]{0:T(512)S(1)}, f32[512,5120]{1,0:T(8,128)}) fusion(f32[5120]{0:T(1024)S(1)} %add_rsqrt_fusion, f32[512]{0:T(512)S(1)} %rsqrt_multiply_fusion, bf16[512,1280]{0,1:T(8,128)(2,1)} %all-gather.2.cloned.1.call-done, bf16[5120,1280]{1,0:T(8,128)(2,1)} %param.4), kind=kOutput, calls=%fused_computation.13 | convolution fusion | flops 6718750208 | bytes 24928256 | tf_op jit(solution)/shard_map/dot_general | solution.py:19
  47.7 0.0 copy-start
  47.7 5.9 %psum.49 = f32[512]{0:T(512)S(1)} all-reduce(f32[512]{0:T(512)S(1)} %get-tuple-element.5), channel_id=1, replica_groups=mesh['shape'=8,'cls'=4] {'cls'}, use_global_device_ids=true, to_apply=%region_3.0 | all-reduce | flops 512 | bytes 4096 | tf_op jit(solution)/shard_map/psum | solution.py:12
  53.5 7.6 %fusion.1 = f32[1,5120]{1,0:T(1,128)S(1)} fusion(f32[512,1]{0,1:T(1,128)S(1)} %bitcast.32, f32[512,5120]{1,0:T(8,128)} %get-tuple-element.6), kind=kOutput, calls=%fused_computation.14 | convolution fusion | flops 31457280 | bytes 10508288 | tf_op jit(solution)/shard_map/dot_general | solution.py:30
  61.2 37.2 %psum.50 = f32[5120]{0:T(1024)S(1)} all-reduce(f32[5120]{0:T(1024)S(1)} %bitcast.27), channel_id=1, replica_groups=mesh['shape'=8,'cls'=4] {'shape'}, use_global_device_ids=true, to_apply=%region_4.0 | all-reduce | flops 5120 | bytes 40960 | tf_op jit(solution)/shard_map/psum | solution.py:31
  98.4 0.0 copy-done
  98.4 11.5 %fusion.2 = f32[1,512]{1,0:T(1,128)S(1)} fusion(f32[512,5120]{1,0:T(8,128)} %get-tuple-element.6, f32[5120,1]{0,1:T(1,128)S(1)} %bitcast.30), kind=kOutput, calls=%fused_computation.15 | convolution fusion | flops 31457280 | bytes 10508288 | tf_op jit(solution)/shard_map/dot_general | solution.py:32
  109.9 5.7 %psum.51 = f32[512]{0:T(512)S(1)} all-reduce(f32[512]{0:T(512)S(1)} %bitcast.33), channel_id=1, replica_groups=mesh['shape'=8,'cls'=4] {'cls'}, use_global_device_ids=true, to_apply=%region_5.0 | all-reduce | flops 512 | bytes 4096 | tf_op jit(solution)/shard_map/psum | solution.py:12
  115.6 7.6 %fusion.3 = f32[1,5120]{1,0:T(1,128)S(1)} fusion(f32[512,1]{0,1:T(1,128)S(1)} %bitcast.34, f32[512,5120]{1,0:T(8,128)} %get-tuple-element.6), kind=kOutput, calls=%fused_computation.16 | convolution fusion | flops 31457280 | bytes 10508288 | tf_op jit(solution)/shard_map/dot_general | solution.py:30
  123.2 33.0 %psum.52 = f32[5120]{0:T(1024)S(1)} all-reduce(f32[5120]{0:T(1024)S(1)} %bitcast.28), channel_id=1, replica_groups=mesh['shape'=8,'cls'=4] {'shape'}, use_global_device_ids=true, to_apply=%region_6.0 | all-reduce | flops 5120 | bytes 40960 | tf_op jit(solution)/shard_map/psum | solution.py:31
  156.2 11.5 %fusion.4 = f32[1,512]{1,0:T(1,128)S(1)} fusion(f32[512,5120]{1,0:T(8,128)} %get-tuple-element.6, f32[5120,1]{0,1:T(1,128)S(1)} %bitcast.31), kind=kOutput, calls=%fused_computation.17 | convolution fusion | flops 31457280 | bytes 10508288 | tf_op jit(solution)/shard_map/dot_general | solution.py:32
  167.7 5.9 %psum.53 = f32[512]{0:T(512)S(1)} all-reduce(f32[512]{0:T(512)S(1)} %bitcast.35), channel_id=1, replica_groups=mesh['shape'=8,'cls'=4] {'cls'}, use_global_device_ids=true, to_apply=%region_7.0 | all-reduce | flops 512 | bytes 4096 | tf_op jit(solution)/shard_map/psum | solution.py:12
  173.6 7.6 %fusion.5 = f32[1,5120]{1,0:T(1,128)S(1)} fusion(f32[512,1]{0,1:T(1,128)S(1)} %bitcast.36, f32[512,5120]{1,0:T(8,128)} %get-tuple-element.6), kind=kOutput, calls=%fused_computation.18 | convolution fusion | flops 31457280 | bytes 10508288 | tf_op jit(solution)/shard_map/dot_general | solution.py:30
  181.2 33.0 %psum.54 = f32[5120]{0:T(1024)S(1)} all-reduce(f32[5120]{0:T(1024)S(1)} %bitcast.29), channel_id=1, replica_groups=mesh['shape'=8,'cls'=4] {'shape'}, use_global_device_ids=true, to_apply=%region_8.0 | all-reduce | flops 5120 | bytes 40960 | tf_op jit(solution)/shard_map/psum | solution.py:31
  214.2 11.5 %fusion.6 = f32[1,512]{1,0:T(1,128)S(1)} fusion(f32[512,5120]{1,0:T(8,128)} %get-tuple-element.6, f32[5120,1]{0,1:T(1,128)S(1)} %bitcast.26), kind=kOutput, calls=%fused_computation.19 | convolution fusion | flops 31457280 | bytes 10508288 | tf_op jit(solution)/shard_map/dot_general | solution.py:32
  225.7 5.7 %psum.55 = f32[512]{0:T(512)S(1)} all-reduce(f32[512]{0:T(512)S(1)} %bitcast.37), channel_id=1, replica_groups=mesh['shape'=8,'cls'=4] {'cls'}, use_global_device_ids=true, to_apply=%region_9.0 | all-reduce | flops 512 | bytes 4096 | tf_op jit(solution)/shard_map/psum | solution.py:12
  231.4 8.0 %multiply_convert_fusion = bf16[512,5120]{1,0:T(8,128)(2,1)} fusion(f32[512,5120]{1,0:T(8,128)} %get-tuple-element.6, f32[5120]{0:T(1024)S(1)} %convert_divide_fusion, f32[512]{0:T(512)S(1)} %broadcast_divide_fusion), kind=kLoop, calls=%fused_computation.1 | loop fusion | flops 7864320 | bytes 15751168 | tf_op jit(solution)/shard_map/convert_element_type | solution.py:34
  (9 shorter events, 0.1 us)
Async XLA Ops:
  6.5 23.3 %all-gather.2.cloned.1.call-start = ((), (), s32[]{:S(2)}) async-start(), calls=%async_computation | async-start | bytes 1638400 | tf_op jit(solution)/shard_map/all_gather | solution.py:18
  47.7 50.7 %copy-start = (s32[5120]{0:T(1024)S(1)}, s32[5120]{0:T(1024)}, u32[]{:S(2)}) copy-start(s32[5120]{0:T(1024)} %param.5) | copy-start | bytes 61444
Sparse Core Ops, SparseCore 0:
  8.9 20.8 all-gather.1
where the time goes:
time: 247 us; the launch traced here: 246 us
  blocking collectives  126 us (51%)
  matrix products  73.5 us (30%)
  other arithmetic  17.1 us (7%)
  waiting for transfers between devices  15.9 us (6%)
  between operations  13.4 us (5%)
    psum x3, blocking collectives, shards(): col_scale = target / lax.psum(column_part, 'shape')  103 us
    dot_general x3, matrix products, shards(): jnp.dot(kernel, col_scale, precision=lax.Precision.HIGHEST)  34.4 us
    psum x4, blocking collectives, row_totals(): return lax.psum(partial_value, 'cls')  23 us
    dot_general x3, matrix products, shards(): column_part = jnp.dot(row_inv, kernel, precision=lax.Precision.HIGHEST)  22.9 us
    dot_general x1, matrix products, shards(): lax.dot_general(piece, classes, (((1,), (1,)), ((), ())), preferred_eleme...  16.2 us
    all_gather x1, waiting for transfers between devices, shards(): piece = lax.all_gather(shapes, 'cls', axis=1, tiled=True)  15.2 us
    convert_element_type x1, other arithmetic, shards(): return result.astype(jnp.bfloat16)  8 us
    reduce_sum x1, other arithmetic, shards(): class_scale = lax.rsqrt(jnp.sum(class_f * class_f, axis=1) + epsilon)  7.35 us
  transfers between devices with their start and end apart: 1, of which 1 were waited for; matrix products, arithmetic and copies ran while one was open for 3% of the time, Pallas kernels for 0%

commit v1 on v0

--- a/solution.py
+++ b/solution.py
@@ -15,7 +15,9 @@
 def shards(shapes, classes, counts):
     class_f = classes.astype(jnp.float32)
     class_scale = lax.rsqrt(jnp.sum(class_f * class_f, axis=1) + epsilon)
-    piece = lax.all_gather(shapes, "cls", axis=1, tiled=True)
+    piece = jnp.concatenate(
+        lax.all_to_all(jnp.stack([shapes] * lax.axis_size("cls")), "cls", 0, 0), axis=1
+    )
     term = lax.dot_general(
         piece, classes, (((1,), (1,)), ((), ())), preferred_element_type=jnp.float32
     )

time: 247 us -> 231 us (0.935)
  between operations: 13.4 us -> 0.02 us
  waiting for transfers between devices: 15.9 us -> 9.88 us
  starting transfers between devices: 0.01 us -> 4.26 us
    all_gather x1 -> x0, waiting for transfers between devices: 15.2 us -> none  [shards(): piece = lax.all_gather(shapes, 'cls', axis=1, tiled=True)]
    all_to_all x0 -> x1, waiting for transfers between devices: none -> 9.88 us  [shards(): lax.all_to_all(jnp.stack([shapes] * lax.axis_size('cls')), 'cls', 0, 0)]
    all_to_all x0 -> x1, starting transfers between devices: none -> 4.26 us  [shards(): lax.all_to_all(jnp.stack([shapes] * lax.axis_size('cls')), 'cls', 0, 0)]
where the time goes in v1:
time: 231 us
  blocking collectives  127 us (55%)
  matrix products  71.3 us (31%)
  other arithmetic  15.8 us (7%)
  waiting for transfers between devices  9.88 us (4%)
  starting transfers between devices  4.26 us (2%)
    psum x3, blocking collectives, shards(): col_scale = target / lax.psum(column_part, 'shape')  104 us
    dot_general x3, matrix products, shards(): jnp.dot(kernel, col_scale, precision=lax.Precision.HIGHEST)  34.4 us
    psum x4, blocking collectives, row_totals(): return lax.psum(partial_value, 'cls')  23.1 us
    dot_general x3, matrix products, shards(): column_part = jnp.dot(row_inv, kernel, precision=lax.Precision.HIGHEST)  22.9 us
    dot_general x1, matrix products, shards(): lax.dot_general(piece, classes, (((1,), (1,)), ((), ())), preferred_eleme...  14 us
    all_to_all x1, waiting for transfers between devices, shards(): lax.all_to_all(jnp.stack([shapes] * lax.axis_size('cls')), 'cls', 0, 0)  9.88 us
    convert_element_type x1, other arithmetic, shards(): return result.astype(jnp.bfloat16)  8 us
    reduce_sum x1, other arithmetic, shards(): class_scale = lax.rsqrt(jnp.sum(class_f * class_f, axis=1) + epsilon)  7.35 us
  transfers between devices with their start and end apart: 1, of which 1 were waited for; matrix products, arithmetic and copies ran while one was open for 3% of the time, Pallas kernels for 0%

profile of v1, /device:TPU:0, one launch (start us, length us, event | category | flops | bytes accessed | tf_op | source)
XLA Modules:
  0.0 230.5 jit_solution(6281954552882883272)
XLA Ops:
  0.0 2.1 stack.2
  2.1 4.3 %all-to-all-start = ((bf16[4,512,320]{1,2,0:T(8,128)(2,1)}), bf16[4,512,320]{1,2,0:T(8,128)(2,1)S(1)}, u32[]{:S(2)}, u32[]{:S(2)}) async-start(bf16[4,512,320]{1,2,0:T(8,128)(2,1)} %stack.2), calls=%async_computation | async-start | bytes 2621440 | tf_op jit(solution)/shard_map/all_to_all | solution.py:19
  6.4 7.3 %multiply_reduce_fusion = f32[5120]{0:T(1024)S(1)} fusion(bf16[5120,1280]{1,0:T(8,128)(2,1)} %param.4), kind=kLoop, calls=%fused_computation | loop fusion | flops 19655680 | bytes 13127680 | tf_op jit(solution)/shard_map/reduce_sum | solution.py:17
  13.8 9.9 %all-to-all-done = bf16[4,512,320]{1,2,0:T(8,128)(2,1)S(1)} async-done(((bf16[4,512,320]{1,2,0:T(8,128)(2,1)}), bf16[4,512,320]{1,2,0:T(8,128)(2,1)S(1)}, u32[]{:S(2)}, u32[]{:S(2)}) %all-to-all-start) | async-done | bytes 1310752 | tf_op jit(solution)/shard_map/all_to_all | solution.py:19
  23.6 0.3 multiply_reduce_fusion.1
  24.0 14.0 %fusion = (f32[512]{0:T(512)S(1)}, f32[512,5120]{1,0:T(8,128)}) fusion(f32[5120]{0:T(1024)S(1)} %add_rsqrt_fusion, f32[512]{0:T(512)S(1)} %rsqrt_multiply_fusion, bf16[512,1280]{0,1:T(8,128)(2,1)S(1)} %bitcast.30, bf16[5120,1280]{1,0:T(8,128)(2,1)} %param.4), kind=kOutput, calls=%fused_computation.13 | convolution fusion | flops 6718750208 | bytes 24928256 | tf_op jit(solution)/shard_map/dot_general | solution.py:21
  38.0 0.0 copy-start
  38.0 5.9 %psum.49 = f32[512]{0:T(512)S(1)} all-reduce(f32[512]{0:T(512)S(1)} %get-tuple-element.5), channel_id=1, replica_groups=mesh['shape'=8,'cls'=4] {'cls'}, use_global_device_ids=true, to_apply=%region_3.0 | all-reduce | flops 512 | bytes 4096 | tf_op jit(solution)/shard_map/psum | solution.py:12
  43.9 7.6 %fusion.1 = f32[1,5120]{1,0:T(1,128)S(1)} fusion(f32[512,1]{0,1:T(1,128)S(1)} %bitcast.37, f32[512,5120]{1,0:T(8,128)} %get-tuple-element.6), kind=kOutput, calls=%fused_computation.14 | convolution fusion | flops 31457280 | bytes 10508288 | tf_op jit(solution)/shard_map/dot_general | solution.py:32
  51.5 38.1 %psum.50 = f32[5120]{0:T(1024)S(1)} all-reduce(f32[5120]{0:T(1024)S(1)} %bitcast.32), channel_id=1, replica_groups=mesh['shape'=8,'cls'=4] {'shape'}, use_global_device_ids=true, to_apply=%region_4.0 | all-reduce | flops 5120 | bytes 40960 | tf_op jit(solution)/shard_map/psum | solution.py:33
  89.6 0.0 copy-done
  89.6 11.5 %fusion.2 = f32[1,512]{1,0:T(1,128)S(1)} fusion(f32[512,5120]{1,0:T(8,128)} %get-tuple-element.6, f32[5120,1]{0,1:T(1,128)S(1)} %bitcast.35), kind=kOutput, calls=%fused_computation.15 | convolution fusion | flops 31457280 | bytes 10508288 | tf_op jit(solution)/shard_map/dot_general | solution.py:34
  101.1 5.7 %psum.51 = f32[512]{0:T(512)S(1)} all-reduce(f32[512]{0:T(512)S(1)} %bitcast.38), channel_id=1, replica_groups=mesh['shape'=8,'cls'=4] {'cls'}, use_global_device_ids=true, to_apply=%region_5.0 | all-reduce | flops 512 | bytes 4096 | tf_op jit(solution)/shard_map/psum | solution.py:12
  106.7 7.6 %fusion.3 = f32[1,5120]{1,0:T(1,128)S(1)} fusion(f32[512,1]{0,1:T(1,128)S(1)} %bitcast.39, f32[512,5120]{1,0:T(8,128)} %get-tuple-element.6), kind=kOutput, calls=%fused_computation.16 | convolution fusion | flops 31457280 | bytes 10508288 | tf_op jit(solution)/shard_map/dot_general | solution.py:32
  114.4 33.0 %psum.52 = f32[5120]{0:T(1024)S(1)} all-reduce(f32[5120]{0:T(1024)S(1)} %bitcast.33), channel_id=1, replica_groups=mesh['shape'=8,'cls'=4] {'shape'}, use_global_device_ids=true, to_apply=%region_6.0 | all-reduce | flops 5120 | bytes 40960 | tf_op jit(solution)/shard_map/psum | solution.py:33
  147.4 11.5 %fusion.4 = f32[1,512]{1,0:T(1,128)S(1)} fusion(f32[512,5120]{1,0:T(8,128)} %get-tuple-element.6, f32[5120,1]{0,1:T(1,128)S(1)} %bitcast.36), kind=kOutput, calls=%fused_computation.17 | convolution fusion | flops 31457280 | bytes 10508288 | tf_op jit(solution)/shard_map/dot_general | solution.py:34
  158.9 5.9 %psum.53 = f32[512]{0:T(512)S(1)} all-reduce(f32[512]{0:T(512)S(1)} %bitcast.40), channel_id=1, replica_groups=mesh['shape'=8,'cls'=4] {'cls'}, use_global_device_ids=true, to_apply=%region_7.0 | all-reduce | flops 512 | bytes 4096 | tf_op jit(solution)/shard_map/psum | solution.py:12
  164.7 7.6 %fusion.5 = f32[1,5120]{1,0:T(1,128)S(1)} fusion(f32[512,1]{0,1:T(1,128)S(1)} %bitcast.41, f32[512,5120]{1,0:T(8,128)} %get-tuple-element.6), kind=kOutput, calls=%fused_computation.18 | convolution fusion | flops 31457280 | bytes 10508288 | tf_op jit(solution)/shard_map/dot_general | solution.py:32
  172.4 33.0 %psum.54 = f32[5120]{0:T(1024)S(1)} all-reduce(f32[5120]{0:T(1024)S(1)} %bitcast.34), channel_id=1, replica_groups=mesh['shape'=8,'cls'=4] {'shape'}, use_global_device_ids=true, to_apply=%region_8.0 | all-reduce | flops 5120 | bytes 40960 | tf_op jit(solution)/shard_map/psum | solution.py:33
  205.4 11.5 %fusion.6 = f32[1,512]{1,0:T(1,128)S(1)} fusion(f32[512,5120]{1,0:T(8,128)} %get-tuple-element.6, f32[5120,1]{0,1:T(1,128)S(1)} %bitcast.31), kind=kOutput, calls=%fused_computation.19 | convolution fusion | flops 31457280 | bytes 10508288 | tf_op jit(solution)/shard_map/dot_general | solution.py:34
  216.9 5.7 %psum.55 = f32[512]{0:T(512)S(1)} all-reduce(f32[512]{0:T(512)S(1)} %bitcast.42), channel_id=1, replica_groups=mesh['shape'=8,'cls'=4] {'cls'}, use_global_device_ids=true, to_apply=%region_9.0 | all-reduce | flops 512 | bytes 4096 | tf_op jit(solution)/shard_map/psum | solution.py:12
  222.5 8.0 %multiply_convert_fusion = bf16[512,5120]{1,0:T(8,128)(2,1)} fusion(f32[512,5120]{1,0:T(8,128)} %get-tuple-element.6, f32[5120]{0:T(1024)S(1)} %convert_divide_fusion, f32[512]{0:T(512)S(1)} %broadcast_divide_fusion), kind=kLoop, calls=%fused_computation.1 | loop fusion | flops 7864320 | bytes 15751168 | tf_op jit(solution)/shard_map/convert_element_type | solution.py:36
  (9 shorter events, 0.1 us)
Async XLA Ops:
  2.1 21.5 %all-to-all-start = ((bf16[4,512,320]{1,2,0:T(8,128)(2,1)}), bf16[4,512,320]{1,2,0:T(8,128)(2,1)S(1)}, u32[]{:S(2)}, u32[]{:S(2)}) async-start(bf16[4,512,320]{1,2,0:T(8,128)(2,1)} %stack.2), calls=%async_computation | async-start | bytes 2621440 | tf_op jit(solution)/shard_map/all_to_all | solution.py:19
  38.0 51.6 %copy-start = (s32[5120]{0:T(1024)S(1)}, s32[5120]{0:T(1024)}, u32[]{:S(2)}) copy-start(s32[5120]{0:T(1024)} %param.5) | copy-start | bytes 61444
